TPU v7x, 128 devices: a whole 4x4x4 slice. The times are simulated.
128 devices in a mesh: lm: 8 (over z, x_hi), sl: 16 (over y, x_lo, core).
Axes of the slice: x: 4 (x_hi: 2, x_lo: 2; x = x_hi * 2 + x_lo), y: 4, z: 4, core: 2. Of those that a mesh axis runs over, the one named last changes fastest.
Arguments:
- slab: bfloat16 [16384, 1024], P('sl'), may hold values from -6 to 6
- landmarks: bfloat16 [32768, 1024], P(('lm', 'sl')), may hold values from -6 to 6
- codes: bfloat16 [32768, 96], P(('lm', 'sl')), may hold values from -4 to 4
- exponents: int32 [256], P(('lm', 'sl')), may hold values from -3 to 3
- eigvec: bfloat16 [96, 64], replicated, may hold values from -0.625 to 0.625
- ritz: float32 [64], replicated, may hold values from 0.5 to 4
Outputs:
- extended: float32 [16384, 64], P('sl')
All inputs are finite; a program needn't handle non-finite values.
Results may differ from a plain program's by a relative error of at most 0.004.
Values may be sent and summed in bfloat16 or wider, within the bound.
A program may use at most 128 MiB of HBM per device.

v0:
```python
import math
import jax
import jax.numpy as jnp
from jax import lax
from jax.sharding import PartitionSpec as P

BLOCK = 128


def local(slab, landmarks, codes, exponents, eigvec, ritz):
    total_land = codes.shape[0] * lax.axis_size("lm") * lax.axis_size("sl")
    coeff = 1.0 / math.sqrt(slab.shape[1])
    factor = 1.0 / (ritz * math.sqrt(total_land))
    scale = jnp.exp2(exponents.astype(jnp.float32))
    rows_scale = jnp.repeat(scale, BLOCK)
    basis = (codes.astype(jnp.float32) * rows_scale[:, None]).astype(jnp.bfloat16)
    vectors = jnp.dot(basis, eigvec, preferred_element_type=jnp.float32).astype(jnp.bfloat16)
    land = lax.all_gather(landmarks, "sl", axis=0, tiled=True)
    vec = lax.all_gather(vectors, "sl", axis=0, tiled=True)
    scores = jnp.dot(slab, land.T, preferred_element_type=jnp.float32) * coeff
    affinity = jnp.exp(scores).astype(jnp.bfloat16)
    terms = jnp.dot(affinity, vec, preferred_element_type=jnp.float32)
    summed = lax.psum(terms, "lm")
    return summed * factor[None, :]


def solution(mesh):
    return jax.shard_map(
        local,
        mesh=mesh,
        in_specs=(
            P("sl", None),
            P(("lm", "sl"), None),
            P(("lm", "sl"), None),
            P(("lm", "sl")),
            P(),
            P(),
        ),
        out_specs=P("sl", None),
        check_vma=False,
    )
```

profile of v0, /device:TPU:0, one launch (start us, length us, event | category | flops | bytes accessed | tf_op | source)
XLA Modules:
  0.0 178.2 jit_solution(8846013648305641239)
XLA Ops:
  6.5 0.0 copy-start
  6.5 0.0 all-gather.2.cloned.1.call-start
  6.5 0.7 all-gather.2.cloned.1.call-update
  7.3 0.0 all-reduce.2.cloned.1.call-start
  7.3 0.7 multiply_exponential_fusion
  8.0 0.1 broadcast_bitcast_fusion
  8.0 1.0 convolution_convert_fusion
  9.0 30.0 %all_gather.7 = bf16[4096,64]{1,0:T(8,128)(2,1)S(1)} all-gather(bf16[256,64]{1,0:T(8,128)(2,1)S(1)} %convolution_convert_fusion), channel_id=1, replica_groups=mesh['lm'=8,'sl'=16] {'sl'}, dimensions={0}, use_global_device_ids=true | all-gather | bytes 557056 | tf_op jit(solution)/shard_map/all_gather | solution.py:19
  39.1 0.0 copy-start.1
  39.1 27.3 %all-gather.2.cloned.1.call-done = bf16[4096,1024]{1,0:T(8,128)(2,1)} async-done(((bf16[256,1024]{1,0:T(8,128)(2,1)}), bf16[4096,1024]{1,0:T(8,128)(2,1)}) %all-gather.2.cloned.1.call-update) | async-done | bytes 8388624 | tf_op jit(solution)/shard_map/all_gather | solution.py:18
  66.4 0.0 copy-done
  66.4 15.6 %fusion.1 = f32[1024,64]{0,1:T(8,128)} fusion(bf16[4096,64]{1,0:T(8,128)(2,1)S(1)} %all_gather.7, bf16[1024,1024]{1,0:T(8,128)(2,1)S(1)} %copy-done, bf16[4096,1024]{1,0:T(8,128)(2,1)} %all-gather.2.cloned.1.call-done), kind=kOutput, calls=%fused_computation.8 | convolution fusion | flops 9135194112 | bytes 11272192 | tf_op jit(solution)/shard_map/dot_general | solution.py:22
  82.0 0.0 all-reduce.2.cloned.1.call-update
  82.0 0.0 copy-done.1
  82.0 87.6 %all-reduce.2.cloned.1.call-done = f32[1024,64]{0,1:T(8,128)} async-done(((f32[1024,64]{0,1:T(8,128)}), f32[1024,64]{0,1:T(8,128)}) %all-reduce.2.cloned.1.call-update) | async-done | bytes 262160 | tf_op jit(solution)/shard_map/psum | solution.py:23
  169.6 1.7 broadcast_multiply_fusion
  (1 shorter events, 0.0 us)
Async XLA Ops:
  6.5 59.8 %copy-start = (bf16[1024,1024]{1,0:T(8,128)(2,1)S(1)}, bf16[1024,1024]{1,0:T(8,128)(2,1)}, u32[]{:S(2)}) copy-start(bf16[1024,1024]{1,0:T(8,128)(2,1)} %param.6) | copy-start | bytes 6291460
  6.5 59.8 %all-gather.2.cloned.1.call-start = ((), (), s32[]{:S(2)}) async-start(), calls=%async_computation | async-start | bytes 8912896 | tf_op jit(solution)/shard_map/all_gather | solution.py:18
  7.3 162.3 %all-reduce.2.cloned.1.call-start = ((), (), s32[]{:S(2)}) async-start(), calls=%async_computation.1 | async-start | bytes 524288 | tf_op jit(solution)/shard_map/psum | solution.py:23
  39.1 42.9 %copy-start.1 = (f32[64]{0:T(128)S(1)}, f32[64]{0:T(128)}, u32[]{:S(2)}) copy-start(f32[64]{0:T(128)} %param.11) | copy-start | bytes 772
Sparse Core Ops, SparseCore 0:
  9.1 57.2 all-gather.1
  82.1 87.4 all-reduce.1
where the time goes:
time: 178 us
  waiting for transfers between devices  116 us (65%)
  blocking collectives  30 us (17%)
  matrix products  16.6 us (9%)
  between operations  13.4 us (8%)
  other arithmetic  2.4 us (1%)
    psum x1, waiting for transfers between devices, local(): summed = lax.psum(terms, 'lm')  87.6 us
    all_gather x1, blocking collectives, local(): vec = lax.all_gather(vectors, 'sl', axis=0, tiled=True)  30 us
    all_gather x1, waiting for transfers between devices, local(): land = lax.all_gather(landmarks, 'sl', axis=0, tiled=True)  27.3 us
    dot_general x1, matrix products, local(): terms = jnp.dot(affinity, vec, preferred_element_type=jnp.float32)  15.6 us
  transfers between devices with their start and end apart: 2, of which 2 were waited for; matrix products, arithmetic and copies ran while one was open for 1% of the time, Pallas kernels for 0%

commit v1 on v0

--- a/solution.py
+++ b/solution.py
@@ -5,6 +5,12 @@
 from jax.sharding import PartitionSpec as P
 
 BLOCK = 128
+number_the_scenes = lambda group_axis, local_block: jnp.concatenate(
+    lax.all_to_all(
+        jnp.stack([local_block for _ in range(lax.psum(1, group_axis))]), group_axis, 0, 0
+    ),
+    axis=0,
+)
 
 
 def local(slab, landmarks, codes, exponents, eigvec, ritz):
@@ -15,7 +21,7 @@
     rows_scale = jnp.repeat(scale, BLOCK)
     basis = (codes.astype(jnp.float32) * rows_scale[:, None]).astype(jnp.bfloat16)
     vectors = jnp.dot(basis, eigvec, preferred_element_type=jnp.float32).astype(jnp.bfloat16)
-    land = lax.all_gather(landmarks, "sl", axis=0, tiled=True)
+    land = number_the_scenes("sl", landmarks)
     vec = lax.all_gather(vectors, "sl", axis=0, tiled=True)
     scores = jnp.dot(slab, land.T, preferred_element_type=jnp.float32) * coeff
     affinity = jnp.exp(scores).astype(jnp.bfloat16)

time: 178 us -> 240 us (1.35)
  blocking collectives: 30 us -> 113 us
  waiting for transfers between devices: 116 us -> 84.3 us
  starting transfers between devices: 0.04 us -> 5.81 us
  local copies, waits for them, and re-layouts: 0.08 us -> 5.58 us
    all_gather x1, blocking collectives: 30 us -> 113 us  [local(): vec = lax.all_gather(vectors, 'sl', axis=0, tiled=True)]
    all_gather x1 -> x0, waiting for transfers between devices: 27.3 us -> none  [local(): land = lax.all_gather(landmarks, 'sl', axis=0, tiled=True)]
    all_to_all x0 -> x1, starting transfers between devices: none -> 5.77 us  [lax.all_to_all(jnp.stack([local_block for _ in range(lax.psum(1, group_ax...]
    another operation x0 -> x1, local copies, waits for them, and re-layouts: none -> 5.49 us  [jnp.stack([local_block for _ in range(lax.psum(1, group_axis))])]
    psum x1, waiting for transfers between devices: 87.6 us -> 84.3 us  [local(): summed = lax.psum(terms, 'lm')]
  transfers between devices with their start and end apart: 2 -> 2, of which waited for: 2 -> 1; matrix products, arithmetic and copies ran while one was open for 1% -> 0% of each run, Pallas kernels for 0% -> 0%
where the time goes in v1:
time: 240 us; the launch traced here: 239 us
  blocking collectives  113 us (47%)
  waiting for transfers between devices  84.3 us (35%)
  matrix products  15.8 us (7%)
  between operations  13.4 us (6%)
  starting transfers between devices  5.81 us (2%)
  local copies, waits for them, and re-layouts  5.58 us (2%)
    all_gather x1, blocking collectives, local(): vec = lax.all_gather(vectors, 'sl', axis=0, tiled=True)  113 us
    psum x1, waiting for transfers between devices, local(): summed = lax.psum(terms, 'lm')  84.3 us
    dot_general x1, matrix products, local(): terms = jnp.dot(affinity, vec, preferred_element_type=jnp.float32)  15.6 us
    all_to_all x1, starting transfers between devices, lax.all_to_all(jnp.stack([local_block for _ in range(lax.psum(1, group_ax...  5.77 us
    another operation x1, local copies, waits for them, and re-layouts, jnp.stack([local_block for _ in range(lax.psum(1, group_axis))])  5.49 us
  transfers between devices with their start and end apart: 2, of which 1 were waited for; matrix products, arithmetic and copies ran while one was open for 0% of the time, Pallas kernels for 0%

profile of v1, /device:TPU:0, one launch (start us, length us, event | category | flops | bytes accessed | tf_op | source)
XLA Modules:
  0.0 239.4 jit_solution(3695207675596308)
XLA Ops:
  6.5 0.0 copy-start
  6.5 5.5 %stack.2 = bf16[16,256,1024]{2,1,0:T(8,128)(2,1)} broadcast(bf16[256,1024]{1,0:T(8,128)(2,1)} %param.7), dimensions={1,2} | broadcast | bytes 8912896 | tf_op jit(solution)/shard_map/stack | solution.py:10
  12.0 0.0 copy-start.3
  12.0 0.0 copy-start.1
  12.0 0.0 copy-start.2
  12.0 5.8 %all-to-all-start = ((bf16[16,256,1024]{2,1,0:T(8,128)(2,1)}), bf16[16,256,1024]{2,1,0:T(8,128)(2,1)}, u32[]{:S(2)}, u32[]{:S(2)}) async-start(bf16[16,256,1024]{2,1,0:T(8,128)(2,1)} %stack.2), calls=%async_computation | async-start | bytes 16777216 | tf_op jit(solution)/shard_map/all_to_all | solution.py:9
  17.8 0.0 all-reduce.2.cloned.1.call-start
  17.9 0.0 copy-done.3
  17.9 0.1 broadcast_bitcast_fusion
  18.0 0.0 copy-done.1
  18.0 0.0 copy-done.2
  18.0 0.2 convolution_convert_fusion
  18.2 112.7 %all_gather.3 = bf16[4096,64]{1,0:T(8,128)(2,1)S(1)} all-gather(bf16[256,64]{1,0:T(8,128)(2,1)S(1)} %convolution_convert_fusion), channel_id=1, replica_groups=mesh['lm'=8,'sl'=16] {'sl'}, dimensions={0}, use_global_device_ids=true | all-gather | bytes 557056 | tf_op jit(solution)/shard_map/all_gather | solution.py:25
  130.8 0.0 all-to-all-done
  130.9 0.0 copy-done
  130.9 0.0 copy-start.4
  130.9 15.6 %fusion.1 = f32[1024,64]{0,1:T(8,128)} fusion(bf16[4096,64]{1,0:T(8,128)(2,1)S(1)} %all_gather.3, bf16[1024,1024]{1,0:T(8,128)(2,1)S(1)} %copy-done, bf16[4096,1024]{1,0:T(8,128)(2,1)} %bitcast), kind=kOutput, calls=%fused_computation.8 | convolution fusion | flops 9135194112 | bytes 11272192 | tf_op jit(solution)/shard_map/dot_general | solution.py:28
  146.5 0.0 all-reduce.2.cloned.1.call-update
  146.5 0.0 copy-done.4
  146.5 84.3 %all-reduce.2.cloned.1.call-done = f32[1024,64]{0,1:T(8,128)} async-done(((f32[1024,64]{0,1:T(8,128)}), f32[1024,64]{0,1:T(8,128)}) %all-reduce.2.cloned.1.call-update) | async-done | bytes 262160 | tf_op jit(solution)/shard_map/psum | solution.py:29
  230.8 1.7 broadcast_multiply_fusion
  (2 shorter events, 0.0 us)
Async XLA Ops:
  6.5 124.3 %copy-start = (bf16[1024,1024]{1,0:T(8,128)(2,1)S(1)}, bf16[1024,1024]{1,0:T(8,128)(2,1)}, u32[]{:S(2)}) copy-start(bf16[1024,1024]{1,0:T(8,128)(2,1)} %param.6) | copy-start | bytes 6291460
  12.0 5.8 %copy-start.3 = (s32[2]{0:T(128)S(1)}, s32[2]{0:T(128)}, u32[]{:S(2)}) copy-start(s32[2]{0:T(128)} %param.9) | copy-start | bytes 28
  12.0 5.9 %copy-start.1 = (bf16[256,96]{0,1:T(8,128)(2,1)S(1)}, bf16[256,96]{0,1:T(8,128)(2,1)}, u32[]{:S(2)}) copy-start(bf16[256,96]{0,1:T(8,128)(2,1)} %param.8) | copy-start | bytes 147460
  12.0 5.9 %copy-start.2 = (bf16[96,64]{0,1:T(8,128)(2,1)S(1)}, bf16[96,64]{0,1:T(8,128)(2,1)}, u32[]{:S(2)}) copy-start(bf16[96,64]{0,1:T(8,128)(2,1)} %param.10) | copy-start | bytes 36868
  12.0 118.8 %all-to-all-start = ((bf16[16,256,1024]{2,1,0:T(8,128)(2,1)}), bf16[16,256,1024]{2,1,0:T(8,128)(2,1)}, u32[]{:S(2)}, u32[]{:S(2)}) async-start(bf16[16,256,1024]{2,1,0:T(8,128)(2,1)} %stack.2), calls=%async_computation | async-start | bytes 16777216 | tf_op jit(solution)/shard_map/all_to_all | solution.py:9
  17.8 213.0 %all-reduce.2.cloned.1.call-start = ((), (), s32[]{:S(2)}) async-start(), calls=%async_computation.1 | async-start | bytes 524288 | tf_op jit(solution)/shard_map/psum | solution.py:29
  130.9 15.6 %copy-start.4 = (f32[64]{0:T(128)S(1)}, f32[64]{0:T(128)}, u32[]{:S(2)}) copy-start(f32[64]{0:T(128)} %param.11) | copy-start | bytes 772
Sparse Core Ops, SparseCore 0:
  146.6 84.1 all-reduce.1
